TPU v7x, 128 devices: a whole 4x4x4 slice. The times are simulated.
128 devices in a mesh: day: 16 (over y_lo, x, core), year: 4 (over z), region: 2 (over y_hi).
Axes of the slice: x: 4, y: 4 (y_hi: 2, y_lo: 2; y = y_hi * 2 + y_lo), z: 4, core: 2. Of those that a mesh axis runs over, the one named last changes fastest.
Arguments:
- samples: bfloat16 [368, 8, 2000, 256], P('day', 'year', 'region'), parts along dimension 2, may hold values from -24 to 24, as said below
- counts: int32 [2, 368, 8], P('region', 'day', 'year'), parts along dimension 0, may hold values from 500 to 1000, as said below
Outputs:
- covariance: float32 [2, 368, 256, 256], P('region', 'day', 'year'), parts along dimension 0
- window_mean: float32 [2, 368, 256], P('region', 'day', 'year'), parts along dimension 0
There are 2 independent parts, one for each index of `region`. A program takes and returns all parts, laid end to end along the dimension named above; each array names one. Nothing has to cross between parts.
Inputs may be any that keep to these rules, and one draw needn't show every extreme that they name: `counts`: every entry lies between 500 and 1000; both ends are taken in every draw. `samples`: finite profile values.
All inputs are finite; a program needn't handle non-finite values.
Results may differ from a plain program's by a relative error of at most 0.0003.
Values sent between devices are 32-bit elements; how exact they have to be, the bound alone decides.
A program may use at most 128 MiB of HBM per device.

v0:
```python
import jax
import jax.numpy as jnp
from jax import lax
from jax.sharding import PartitionSpec as P

HALF = 7


def extended(cells, sides, width):
    for axis, dim in sides:
        count = lax.axis_size(axis)
        head = lax.slice_in_dim(cells, 0, width, axis=dim)
        tail = lax.slice_in_dim(cells, cells.shape[dim] - width, cells.shape[dim], axis=dim)
        cells = jnp.concatenate(
            [
                lax.ppermute(tail, axis, [(i, (i + 1) % count) for i in range(count)]),
                cells,
                lax.ppermute(head, axis, [((i + 1) % count, i) for i in range(count)]),
            ],
            axis=dim,
        )
    return cells


def window_total(padded, days):
    total = padded[0:days]
    for offset in range(1, 2 * HALF + 1):
        total = total + padded[offset : offset + days]
    return total


def shards(samples, counts):
    days, groups, slots, width = samples.shape
    parts_year = lax.axis_size("year")
    share = width // parts_year
    slot_index = lax.broadcasted_iota(jnp.int32, (days, groups, slots), 2)
    valid = slot_index < counts[0][:, :, None]
    masked = jnp.where(valid[..., None], samples, jnp.zeros_like(samples))
    day_gram = jnp.einsum("dgsf,dgsh->dfh", masked, masked, preferred_element_type=jnp.float32)
    day_sum = jnp.sum(masked, axis=(1, 2), dtype=jnp.float32)
    day_count = jnp.sum(counts[0], axis=1).astype(jnp.float32)
    extra = jnp.zeros((days, 8, width), jnp.float32)
    extra = extra.at[:, 0, :].set(day_sum)
    extra = extra.at[:, 1, :].set(jnp.broadcast_to(day_count[:, None], (days, width)))
    blocks = day_gram.reshape(days, parts_year, share, width)
    extra_all = jnp.broadcast_to(extra[:, None], (days, parts_year, 8, width))
    stacked = jnp.concatenate([blocks, extra_all], axis=2).reshape(
        days, parts_year * (share + 8), width
    )
    padded = extended(stacked, (("day", 0),), HALF)
    windowed = window_total(padded, days)
    merged = lax.psum_scatter(windowed, "year", scatter_dimension=1, tiled=True)
    win_gram = merged[:, :share, :]
    win_sum = merged[:, share, :]
    win_count = merged[:, share + 1, 0]
    full_mean = win_sum / win_count[:, None]
    start = lax.axis_index("year") * share
    own_mean = lax.dynamic_slice_in_dim(full_mean, start, share, 1)
    outer = win_count[:, None, None] * own_mean[:, :, None] * full_mean[:, None, :]
    covariance = (win_gram - outer) / (win_count - 1.0)[:, None, None]
    return (covariance[None], own_mean[None])


def solution(mesh):
    placed = (P("day", "year", "region", None), P("region", "day", "year"))
    return jax.shard_map(
        shards,
        mesh=mesh,
        in_specs=placed,
        out_specs=(P("region", "day", "year", None), P("region", "day", "year")),
        check_vma=False,
    )
```

profile of v0, /device:TPU:0, one launch (start us, length us, event | category | flops | bytes accessed | tf_op | source)
XLA Modules:
  0.0 215.6 jit_solution(11842195410273633986)
XLA Ops:
  7.2 0.0 reduce-scatter.2.cloned.1.call-start
  7.2 0.8 copy.5
  8.0 0.2 iota_compare_fusion
  8.2 16.5 %broadcast_select_fusion.6 = bf16[23,2,1000,256]{3,2,1,0:T(8,128)(2,1)} fusion(bf16[23,2,1000,256]{3,2,1,0:T(8,128)(2,1)} %param.6, pred[23,2,1000]{2,1,0:T(4,128)(4,1)S(1)} %iota_compare_fusion), kind=kLoop, calls=%fused_computation.1.clone.1.clone.2 | loop fusion | flops 11776000 | bytes 47150000 | tf_op jit(solution)/shard_map/dgsf,dgsh->dfh/dot_general | solution.py:39
  24.6 6.6 %copy-done = bf16[23,2,1000,256]{3,2,1,0:T(8,128)(2,1)S(1)} copy-done((bf16[23,2,1000,256]{3,2,1,0:T(8,128)(2,1)S(1)}, bf16[23,2,1000,256]{3,2,1,0:T(8,128)(2,1)}, u32[]{:S(2)}) %copy-start) | copy-done | bytes 23552024
  31.2 11.0 %convert_reduce_fusion = f32[23,256]{1,0:T(8,128)S(1)} fusion(bf16[23,2,1000,256]{3,2,1,0:T(8,128)(2,1)S(1)} %copy-done, pred[23,2,1000]{2,1,0:T(4,128)(4,1)S(1)} %iota_compare_fusion), kind=kLoop, calls=%fused_computation | loop fusion | flops 35322112 | bytes 23621552 | tf_op jit(solution)/shard_map/reduce_sum | solution.py:40
  42.2 0.0 copy-start.1
  42.2 19.5 %fusion = f32[23,256,256,1]{2,1,3,0:T(8,128)} fusion(bf16[23,2,1000,256]{3,2,1,0:T(8,128)(2,1)} %broadcast_select_fusion.6), kind=kOutput, calls=%fused_computation.14 | convolution fusion | flops 6029312000 | bytes 29581312 | tf_op jit(solution)/shard_map/dgsf,dgsh->dfh/dot_general | solution.py:39
  61.8 0.1 broadcast_in_dim.20
  61.9 0.1 scatter.9
  62.0 0.1 broadcast_in_dim.21
  62.1 2.6 %fusion.28 = (f32[7,4,72,256]{3,2,1,0:T(8,128)S(1)}, f32[7,4,72,256]{3,2,1,0:T(8,128)S(1)}) fusion(f32[23,4,64,256]{3,2,1,0:T(8,128)} %bitcast.15, f32[23,4,8,256]{3,2,1,0:T(8,128)S(1)} %broadcast_in_dim.21), kind=kLoop, calls=%fused_computation.61 | loop fusion | flops 1032192 | bytes 10911744 | tf_op jit(solution)/shard_map/concatenate | solution.py:47
  64.6 0.1 collective-permute-start
  64.7 3.8 %collective-permute-start.1 = (f32[7,288,256]{2,1,0:T(8,128)S(1)}, f32[7,288,256]{2,1,0:T(8,128)}, u32[]{:S(2)}, u32[]{:S(2)}) collective-permute-start(f32[7,288,256]{2,1,0:T(8,128)S(1)} %bitcast.20), channel_id=1, source_target_pairs={{8,0},{16,8},{24,16},{32,24},{40,32},{48,40},{56,48},{64,56},{72,6... | collective-permute-start | bytes 6193160 | tf_op jit(solution)/shard_map/ppermute | solution.py:18
  68.6 3.7 %pad_maximum_fusion = f32[23,4,72,256]{3,2,1,0:T(8,128)} fusion(f32[23,4,8,256]{3,2,1,0:T(8,128)S(1)} %broadcast_in_dim.21, f32[23,4,64,256]{3,2,1,0:T(8,128)S(1)} %bitcast.18), kind=kLoop, calls=%fused_computation.17 | loop fusion | flops 1695744 | bytes 13565952 | tf_op jit(solution)/shard_map/concatenate | solution.py:47
  72.2 19.8 %collective-permute-done = f32[7,288,256]{2,1,0:T(8,128)} collective-permute-done((f32[7,288,256]{2,1,0:T(8,128)S(1)}, f32[7,288,256]{2,1,0:T(8,128)}, u32[]{:S(2)}, u32[]{:S(2)}) %collective-permute-start) | collective-permute-done | bytes 2064416 | tf_op jit(solution)/shard_map/ppermute | solution.py:16
  92.0 39.5 %fusion.4 = f32[23,288,256]{2,1,0:T(8,128)} fusion(f32[23,288,256]{2,1,0:T(8,128)} %bitcast.19, f32[7,288,256]{2,1,0:T(8,128)} %collective-permute-done.1, f32[7,288,256]{2,1,0:T(8,128)} %collective-permute-done), kind=kLoop, calls=%fused_computation.33 | loop fusion | flops 47480832 | bytes 17694720 | tf_op jit(solution)/shard_map/add | solution.py:28
  131.5 0.0 reduce-scatter.2.cloned.1.call-update
  131.5 71.5 %reduce-scatter.2.cloned.1.call-done = f32[23,72,256]{2,1,0:T(8,128)} async-done(((f32[23,288,256]{2,1,0:T(8,128)}), f32[23,72,256]{2,1,0:T(8,128)}) %reduce-scatter.2.cloned.1.call-update) | async-done | bytes 1695760 | tf_op jit(solution)/shard_map/reduce_scatter | solution.py:52
  203.1 1.1 slice_reduce_fusion
  204.2 1.0 fusion.33
  205.3 0.1 broadcast_multiply_fusion
  205.3 0.6 broadcast_in_dim.39
  206.0 2.8 %fusion.31 = f32[1,23,64,256]{3,2,1,0:T(8,128)} fusion(f32[23,72,256]{2,1,0:T(8,128)} %reduce-scatter.2.cloned.1.call-done, f32[23]{0:T(128)S(1)} %get-tuple-element.27, f32[23,256]{1,0:T(8,128)S(1)} %get-tuple-element.34, f32[23,64]{1,0:T(8,128)S(1)} %get-tuple-element.28), kind=kLoop, calls=%fused_computation.65 | loop fusion | flops 1130496 | bytes 3044188 | tf_op jit(solution)/shard_map/broadcast_in_dim | solution.py:61
  (13 shorter events, 0.1 us)
Async XLA Ops:
  7.2 195.9 %reduce-scatter.2.cloned.1.call-start = ((), (), s32[]{:S(2)}) async-start(), calls=%async_computation.1 | async-start | bytes 8478720 | tf_op jit(solution)/shard_map/reduce_scatter | solution.py:52
  8.2 23.1 %copy-start = (bf16[23,2,1000,256]{3,2,1,0:T(8,128)(2,1)S(1)}, bf16[23,2,1000,256]{3,2,1,0:T(8,128)(2,1)}, u32[]{:S(2)}) copy-start(bf16[23,2,1000,256]{3,2,1,0:T(8,128)(2,1)} %param.6) | copy-start | bytes 70656000
  42.2 19.5 %copy-start.1 = (s32[1,23,2]{1,2,0:T(2,128)S(1)}, s32[1,23,2]{1,2,0:T(2,128)}, u32[]{:S(2)}) copy-start(s32[1,23,2]{1,2,0:T(2,128)} %param.7) | copy-start | bytes 556
  61.7 6.9 %slice-start = ((s8[6029312]{0:T(1024)(128)(4,1)}), s8[1835008]{0:T(1024)(128)(4,1)S(1)}, s32[]{:S(2)}) async-start(s8[6029312]{0:T(1024)(128)(4,1)} %bitcast.16), calls=%async_computation.2 | async-start | bytes 3670016
  62.1 6.5 %slice-start.1 = ((s8[6029312]{0:T(1024)(128)(4,1)}), s8[4194304]{0:T(1024)(128)(4,1)S(1)}, s32[]{:S(2)}) async-start(s8[6029312]{0:T(1024)(128)(4,1)} %bitcast.16), calls=%async_computation.3 | async-start | bytes 8388608
  64.6 27.4 %collective-permute-start = (f32[7,288,256]{2,1,0:T(8,128)S(1)}, f32[7,288,256]{2,1,0:T(8,128)}, u32[]{:S(2)}, u32[]{:S(2)}) collective-permute-start(f32[7,288,256]{2,1,0:T(8,128)S(1)} %bitcast.21), channel_id=1, source_target_pairs={{0,8},{8,16},{16,24},{24,32},{32,40},{40,48},{48,56},{56,64},{64,7... | collective-permute-start | bytes 6193160 | tf_op jit(solution)/shard_map/ppermute | solution.py:16
  64.7 27.3 %collective-permute-start.1 = (f32[7,288,256]{2,1,0:T(8,128)S(1)}, f32[7,288,256]{2,1,0:T(8,128)}, u32[]{:S(2)}, u32[]{:S(2)}) collective-permute-start(f32[7,288,256]{2,1,0:T(8,128)S(1)} %bitcast.20), channel_id=1, source_target_pairs={{8,0},{16,8},{24,16},{32,24},{40,32},{48,40},{56,48},{64,56},{72,6... | collective-permute-start | bytes 6193160 | tf_op jit(solution)/shard_map/ppermute | solution.py:18
Sparse Core Ops, SparseCore 0:
  131.7 71.3 reduce-scatter.1
where the time goes:
time: 217 us; the launch traced here: 216 us
  waiting for transfers between devices  91.4 us (42%)
  other arithmetic  78.4 us (36%)
  matrix products  19.5 us (9%)
  between operations  14.2 us (7%)
  local copies, waits for them, and re-layouts  8.29 us (4%)
  starting transfers between devices  3.95 us (2%)
    reduce_scatter x1, waiting for transfers between devices, shards(): merged = lax.psum_scatter(windowed, 'year', scatter_dimension=1, tiled=True)  71.5 us
    add x1, other arithmetic, window_total(): total = total + padded[offset:offset + days]  39.5 us
    ppermute x1, waiting for transfers between devices, extended(): lax.ppermute(tail, axis, [(i, (i + 1) % count) for i in range(count)])  19.8 us
    dot_general x1, matrix products, shards(): jnp.einsum('dgsf,dgsh->dfh', masked, masked, preferred_element_type=jnp.f...  19.5 us
    dot_general x1, other arithmetic, shards(): jnp.einsum('dgsf,dgsh->dfh', masked, masked, preferred_element_type=jnp.f...  16.5 us
    reduce_sum x1, other arithmetic, shards(): day_sum = jnp.sum(masked, axis=(1, 2), dtype=jnp.float32)  11 us
    unnamed x9, local copies, waits for them, and re-layouts  6.61 us
    concatenate x2, other arithmetic, shards(): jnp.concatenate([blocks, extra_all], axis=2)  6.23 us
  transfers between devices with their start and end apart: 3, of which 2 were waited for; matrix products, arithmetic and copies ran while one was open for 2% of the time, Pallas kernels for 0%

commit v1 on v0

v1 whole, which is shorter than its diff:
```python
import functools

import jax
import jax.numpy as jnp
from jax import lax
from jax.experimental import pallas as pl
from jax.experimental.pallas import tpu as pltpu
from jax.sharding import PartitionSpec as P

HALF = 7
SLOTS = 4
AHEAD = 3
MESH = pl.DeviceIdType.MESH


def kernel(
    low,
    cnt,
    x_ref,
    out_ref,
    win_ref,
    xbuf,
    gram,
    hop,
    ext,
    acc,
    own_s,
    got_s,
    near_s,
    ext_s,
    x_sem,
    o_sem,
    w_sem,
    hop_send,
    hop_recv,
    halo_send,
    halo_recv,
    sum_send,
    sum_recv,
    near_send,
    near_recv,
):
    days, groups, slots, width = x_ref.shape
    z = lax.axis_index("year")
    q = lax.axis_index("day")
    nz = lax.axis_size("year")
    nq = lax.axis_size("day")
    share = width // nz
    after = {"day": lax.rem(q + 1, nq)}
    before = {"day": lax.rem(q + nq - 1, nq)}

    barrier = pltpu.get_barrier_semaphore()
    for j in range(1, nz):
        pl.semaphore_signal(
            barrier, inc=1, device_id={"year": lax.rem(z + j, nz)}, device_id_type=MESH
        )
    pl.semaphore_signal(barrier, inc=1, device_id=after, device_id_type=MESH)
    pl.semaphore_signal(barrier, inc=1, device_id=before, device_id_type=MESH)

    def day_of(i):
        return lax.rem(i + days - HALF, days)

    def step_of(i):
        return 1 + (nz - 2) * lax.rem(i + q, 2)

    def fetch(i):
        slot = lax.rem(i, SLOTS)
        return pltpu.make_async_copy(x_ref.at[day_of(i)], xbuf.at[slot], x_sem.at[slot])

    for i in range(AHEAD):
        fetch(i).start()
    own_s[...] = jnp.zeros_like(own_s)
    pl.semaphore_wait(barrier, nz + 1)

    def block_rows(i, k):
        b = lax.rem(z + (nz - step_of(i)) * (k + 1), nz)
        return pl.ds(pl.multiple_of(b * share, share), share)

    def send(i, k):
        src = gram.at[i, block_rows(i, 0)] if k == 0 else hop.at[k - 1, i]
        return pltpu.make_async_remote_copy(
            src_ref=src,
            dst_ref=hop.at[k, i],
            send_sem=hop_send.at[k, i],
            recv_sem=hop_recv.at[k, i],
            device_id={"year": lax.rem(z + step_of(i), nz)},
            device_id_type=MESH,
        )

    def compute(i):
        slot = lax.rem(i, SLOTS)
        t = day_of(i)
        fetch(i).wait()

        @pl.when(i + AHEAD < days)
        def _():
            fetch(i + AHEAD).start()

        total = jnp.zeros((width, width), jnp.float32)
        sums = jnp.zeros((8, width), jnp.float32)
        count = jnp.int32(0)
        for g in range(groups):
            c = cnt[0, t, g]
            count = count + c
            head = xbuf[slot, g, 0:low, :]
            tail = xbuf[slot, g, low:slots, :]
            rows = low + lax.broadcasted_iota(jnp.int32, tail.shape, 0)
            tail = jnp.where(rows < c, tail, jnp.zeros_like(tail))
            for part in (head, tail):
                total = total + lax.dot_general(
                    part, part, (((0,), (0,)), ((), ())), preferred_element_type=jnp.float32
                )
                ones = jnp.ones((8, part.shape[0]), part.dtype)
                sums = sums + jnp.dot(ones, part, preferred_element_type=jnp.float32)
        gram[i] = total
        mine = lax.broadcasted_iota(jnp.int32, (24, width), 0) == t
        own_s[:, 0:width] = jnp.where(mine, sums[0:1], own_s[:, 0:width])
        counted = jnp.full((24, 128), count, jnp.int32).astype(jnp.float32)
        own_s[:, width:] = jnp.where(mine[:, :128], counted, own_s[:, width:])

    def advance(i, k):
        send(i, k - 1).wait_recv()
        hop[k - 1, i] = hop[k - 1, i] + gram[i, block_rows(i, k)]
        send(i, k).start()

    def first(i, carry):
        compute(i)
        send(i, 0).start()
        return carry

    lax.fori_loop(0, days, first, 0)

    def share_sums(j):
        return pltpu.make_async_remote_copy(
            src_ref=own_s,
            dst_ref=got_s.at[j - 1],
            send_sem=sum_send.at[j - 1],
            recv_sem=sum_recv.at[j - 1],
            device_id={"year": lax.rem(z + j, nz)},
            device_id_type=MESH,
        )

    for j in range(1, nz):
        share_sums(j).start()

    def second(i, carry):
        advance(i, 1)
        return carry

    lax.fori_loop(0, days, second, 0)

    for j in range(1, nz):
        share_sums(j).wait()
    merged = own_s[...]
    for j in range(1, nz):
        merged = merged + got_s[j - 1]
    last = days - HALF
    ext_s[...] = jnp.zeros_like(ext_s)
    ext_s[HALF : HALF + days] = merged[0:days]
    own_s[...] = merged

    def near(side):
        rows = pl.ds(last if side == 0 else 0, 8)
        return pltpu.make_async_remote_copy(
            src_ref=own_s.at[rows],
            dst_ref=near_s.at[side],
            send_sem=near_send.at[side],
            recv_sem=near_recv.at[side],
            device_id=after if side == 0 else before,
            device_id_type=MESH,
        )

    def third(i, carry):
        advance(i, 2)
        return carry

    lax.fori_loop(0, days, third, 0)
    for side in range(2):
        near(side).start()

    def halo(i, to_after):
        t = day_of(i)
        return pltpu.make_async_remote_copy(
            src_ref=ext.at[t + HALF],
            dst_ref=ext.at[t - last if to_after else t + HALF + days],
            send_sem=halo_send.at[i],
            recv_sem=halo_recv.at[i],
            device_id=after if to_after else before,
            device_id_type=MESH,
        )

    def finish(i):
        send(i, 2).wait_recv()
        ext[day_of(i) + HALF] = hop[2, i] + gram[i, block_rows(i, 3)]

    def edge_after(i, carry):
        finish(i)
        halo(i, True).start()
        return carry

    def edge_before(i, carry):
        finish(i)
        halo(i, False).start()
        return carry

    def inner(i, carry):
        finish(i)
        return carry

    lax.fori_loop(0, HALF, edge_after, 0)
    lax.fori_loop(HALF, 2 * HALF, edge_before, 0)
    lax.fori_loop(2 * HALF, days, inner, 0)

    for side in range(2):
        near(side).wait()
    ext_s[0:HALF] = near_s[0, 0:HALF]
    ext_s[HALF + days : 2 * HALF + days] = near_s[1, 0:HALF]
    win = ext_s[0:24]
    for k in range(1, 2 * HALF + 1):
        win = win + ext_s[k : k + 24]
    own_s[...] = win
    win_copy = pltpu.make_async_copy(own_s, win_ref, w_sem)
    win_copy.start()

    def wait_after(i, carry):
        halo(i, True).wait()
        return carry

    def wait_before(i, carry):
        halo(i, False).wait()
        return carry

    lax.fori_loop(0, HALF, wait_after, 0)
    lax.fori_loop(HALF, 2 * HALF, wait_before, 0)

    def window(d, carry):
        total = ext[d]
        for k in range(1, 2 * HALF + 1):
            total = total + ext[d + k]
        acc[d] = total
        return carry

    lax.fori_loop(0, days, window, 0)
    whole = pltpu.make_async_copy(acc, out_ref, o_sem)
    whole.start()

    def drain(i, carry):
        for k in range(nz - 1):
            send(i, k).wait_send()
        return carry

    lax.fori_loop(0, days, drain, 0)
    win_copy.wait()
    whole.wait()


def shards(samples, counts):
    days, groups, slots, width = samples.shape
    nz = lax.axis_size("year")
    share = width // nz
    low = slots // 2 // 16 * 16
    f32 = jnp.float32
    dma = pltpu.SemaphoreType.DMA
    gram, win = pl.pallas_call(
        functools.partial(kernel, low),
        out_shape=(
            jax.ShapeDtypeStruct((days, share, width), f32),
            jax.ShapeDtypeStruct((24, width + 128), f32),
        ),
        in_specs=[
            pl.BlockSpec(memory_space=pltpu.SMEM),
            pl.BlockSpec(memory_space=pl.ANY),
        ],
        out_specs=(pl.BlockSpec(memory_space=pl.ANY), pl.BlockSpec(memory_space=pl.ANY)),
        scratch_shapes=[
            pltpu.VMEM((SLOTS, groups, slots, width), samples.dtype),
            pltpu.VMEM((days, width, width), f32),
            pltpu.VMEM((nz - 1, days, share, width), f32),
            pltpu.VMEM((days + 2 * HALF, share, width), f32),
            pltpu.VMEM((days, share, width), f32),
            pltpu.VMEM((24, width + 128), f32),
            pltpu.VMEM((nz - 1, 24, width + 128), f32),
            pltpu.VMEM((2, 8, width + 128), f32),
            pltpu.VMEM((40, width + 128), f32),
            dma((SLOTS,)),
            dma,
            dma,
            dma((nz - 1, days)),
            dma((nz - 1, days)),
            dma((2 * HALF,)),
            dma((2 * HALF,)),
            dma((nz - 1,)),
            dma((nz - 1,)),
            dma((2,)),
            dma((2,)),
        ],
        compiler_params=pltpu.CompilerParams(
            collective_id=0, has_side_effects=True, vmem_limit_bytes=56 * 2**20
        ),
    )(counts, samples)
    win_sum = win[:days, :width]
    win_count = win[:days, width]
    full_mean = win_sum / win_count[:, None]
    start = lax.axis_index("year") * share
    own_mean = lax.dynamic_slice_in_dim(full_mean, start, share, 1)
    outer = win_count[:, None, None] * own_mean[:, :, None] * full_mean[:, None, :]
    covariance = (gram - outer) / (win_count - 1.0)[:, None, None]
    return (covariance[None], own_mean[None])


def solution(mesh):
    placed = (P("day", "year", "region", None), P("region", "day", "year"))
    return jax.shard_map(
        shards,
        mesh=mesh,
        in_specs=placed,
        out_specs=(P("region", "day", "year", None), P("region", "day", "year")),
        check_vma=False,
    )
```

time: 217 us -> 70.9 us (0.33)
  waiting for transfers between devices: 91.4 us -> 0 us
  other arithmetic: 78.4 us -> 3.73 us
  Pallas kernels: 0 us -> 63.4 us
  matrix products: 19.5 us -> 0 us
  between operations: 14.2 us -> 0.65 us
  local copies, waits for them, and re-layouts: 8.29 us -> 2.79 us
  starting transfers between devices: 3.95 us -> 0 us
    reduce_scatter x1 -> x0, waiting for transfers between devices: 71.5 us -> none  [shards(): merged = lax.psum_scatter(windowed, 'year', scatter_dimension=1, tiled=True)]
    pallas_call x0 -> x1, Pallas kernels: none -> 63.4 us  [shards(): pl.pallas_call(functools.partial(kernel, low), out_shape=(jax.ShapeDtypeS...]
    add x1 -> x0, other arithmetic: 39.5 us -> none  [window_total(): total = total + padded[offset:offset + days]]
    ppermute x2 -> x0, waiting for transfers between devices: 19.8 us -> none  [the longest x1 19.8 us: extended(): lax.ppermute(tail, axis, [(i, (i + 1) % count) for i in range(count)])]
    dot_general x1 -> x0, matrix products: 19.5 us -> none  [shards(): jnp.einsum('dgsf,dgsh->dfh', masked, masked, preferred_element_type=jnp.f...]
    dot_general x1 -> x0, other arithmetic: 16.5 us -> none  [shards(): jnp.einsum('dgsf,dgsh->dfh', masked, masked, preferred_element_type=jnp.f...]
    reduce_sum x2 -> x0, other arithmetic: 11 us -> none  [the longest x1 11 us: shards(): day_sum = jnp.sum(masked, axis=(1, 2), dtype=jnp.float32)]
    concatenate x2 -> x0, other arithmetic: 6.23 us -> none  [shards(): jnp.concatenate([blocks, extra_all], axis=2)]
  transfers between devices with their start and end apart: 3 -> 0, of which waited for: 2 -> 0; matrix products, arithmetic and copies ran while one was open for 2% -> 0% of each run, Pallas kernels for 0% -> 0%
where the time goes in v1:
time: 70.9 us; the launch traced here: 70.6 us
  Pallas kernels  63.4 us (89%)
  other arithmetic  3.73 us (5%)
  local copies, waits for them, and re-layouts  2.79 us (4%)
    pallas_call x1, Pallas kernels, shards(): pl.pallas_call(functools.partial(kernel, low), out_shape=(jax.ShapeDtypeS...  63.4 us
    broadcast_in_dim x1, other arithmetic, shards(): return (covariance[None], own_mean[None])  2.84 us

profile of v1, /device:TPU:0, one launch (start us, length us, event | category | flops | bytes accessed | tf_op | source)
XLA Modules:
  0.0 70.6 jit_solution(1183620548448525049)
XLA Ops:
  0.6 1.4 %copy.5.cnt = s32[1,23,2]{2,1,0:T(8,128)} copy(s32[1,23,2]{1,2,0:T(2,128)} %param.3) | data formatting | bytes 368 | tf_op args[1]
  2.0 63.4 %shard_map.41 = (f32[23,64,256]{2,1,0:T(8,128)}, f32[24,384]{1,0:T(8,128)}) custom-call(s32[1,23,2]{2,1,0:T(8,128)} %copy.5.cnt, bf16[23,2,1000,256]{3,2,1,0:T(8,128)(2,1)} %x_ref.1), custom_call_target="tpu_custom_call" | custom-call | tf_op jit(solution)/shard_map/pallas_call | solution.py:264
  65.4 0.8 %slice_reduce_fusion = f32[23]{0:T(128)S(1)} fusion(f32[24,384]{1,0:T(8,128)} %get-tuple-element.5), kind=kLoop, calls=%fused_computation.2 | loop fusion | bytes 184 | tf_op jit(solution)/shard_map/slice | solution.py:302
  66.2 0.8 %slice_divide_fusion = f32[23,256]{1,0:T(8,128)S(1)} fusion(f32[24,384]{1,0:T(8,128)} %get-tuple-element.5, f32[23]{0:T(128)S(1)} %slice_reduce_fusion), kind=kLoop, calls=%fused_computation.1 | loop fusion | flops 5888 | bytes 47196 | tf_op jit(solution)/shard_map/div | solution.py:303
  67.1 0.1 broadcast_multiply_fusion
  67.1 2.8 %divide_bitcast_fusion = f32[1,23,64,256]{3,2,1,0:T(8,128)} fusion(f32[23,64,256]{2,1,0:T(8,128)} %get-tuple-element.4, f32[23]{0:T(128)S(1)} %broadcast_add_fusion, f32[23,256]{1,0:T(8,128)S(1)} %slice_divide_fusion, f32[23,64]{1,0:T(8,128)S(1)} %get-tuple-element.6), kind=kLoop, calls=%fused_computation | loop fusion | flops 1130496 | bytes 3044188 | tf_op jit(solution)/shard_map/broadcast_in_dim | solution.py:308
  70.0 0.6 broadcast_in_dim.10
  (1 shorter events, 0.0 us)

commit v2 on v1

v2 whole, which is shorter than its diff:
```python
import functools

import jax
import jax.numpy as jnp
from jax import lax
from jax.experimental import pallas as pl
from jax.experimental.pallas import tpu as pltpu
from jax.sharding import PartitionSpec as P

HALF = 7
SPAN = 2 * HALF + 1
SLOTS = 4
AHEAD = 3
LANES = 128
LAG1 = 4
LAG3 = 3
LAG4 = 6
LAG5 = 11
MESH = pl.DeviceIdType.MESH


def turned(x):
    return pltpu.roll(x, LANES // 2, 1)


def flipped(x):
    return jnp.concatenate([x, x], axis=0).T


def kernel(
    low,
    cnt_ref,
    x_ref,
    out_ref,
    mean_ref,
    cnt,
    xbuf,
    pack,
    hop,
    give,
    take,
    tile,
    ext,
    acc,
    own_s,
    got_s,
    mrg_s,
    near_s,
    ext_s,
    mean_s,
    inv_s,
    own_m,
    c_sem,
    x_sem,
    o_sem,
    m_sem,
    hop_send,
    hop_recv,
    give_send,
    give_recv,
    halo_send,
    halo_recv,
    sum_send,
    sum_recv,
    near_send,
    near_recv,
):
    days, groups, slots, width = x_ref.shape
    f32 = jnp.float32
    z = lax.axis_index("year")
    q = lax.axis_index("day")
    nz = lax.axis_size("year")
    nq = lax.axis_size("day")
    share = width // nz
    quarter = share // nz
    rows = share + quarter
    low32 = share // 2
    last = days - HALF
    even = lax.rem(z, 2) == 0
    after = {"day": lax.rem(q + 1, nq)}
    before = {"day": lax.rem(q + nq - 1, nq)}

    def peer(j):
        return {"year": lax.rem(z + j, nz)}

    def left(n):
        return lax.broadcasted_iota(jnp.int32, (n, LANES), 1) < LANES // 2

    barrier = pltpu.get_barrier_semaphore()
    for j in range(1, nz):
        pl.semaphore_signal(barrier, inc=1, device_id=peer(j), device_id_type=MESH)
    pl.semaphore_signal(barrier, inc=1, device_id=after, device_id_type=MESH)
    pl.semaphore_signal(barrier, inc=1, device_id=before, device_id_type=MESH)

    def day_of(i):
        return lax.rem(i + last, days)

    def step_of(i):
        return 1 + (nz - 2) * lax.rem(i + q, 2)

    def fetch(i):
        slot = lax.rem(i, SLOTS)
        return pltpu.make_async_copy(x_ref.at[day_of(i)], xbuf.at[slot], x_sem.at[slot])

    counted = pltpu.make_async_copy(cnt_ref, cnt, c_sem)
    counted.start()
    for i in range(AHEAD):
        fetch(i).start()
    own_s[...] = jnp.zeros_like(own_s)
    ext_s[...] = jnp.zeros_like(ext_s)

    def clear(e, carry):
        acc[e] = jnp.zeros((share, width), f32)
        return carry

    lax.fori_loop(0, days + 4 * HALF, clear, 0)
    counted.wait()

    def compute(i):
        slot = lax.rem(i, SLOTS)
        t = day_of(i)
        fetch(i).wait()

        @pl.when(i + AHEAD < days)
        def _():
            fetch(i + AHEAD).start()

        total = jnp.zeros((width, width), f32)
        sums = jnp.zeros((8, width), f32)
        count = jnp.int32(0)
        for g in range(groups):
            c = cnt[g, t]
            count = count + c
            head = xbuf[slot, g, 0:low, :]
            tail = xbuf[slot, g, low:slots, :]
            at = low + lax.broadcasted_iota(jnp.int32, tail.shape, 0)
            tail = jnp.where(at < c, tail, jnp.zeros_like(tail))
            for part in (head, tail):
                total = total + lax.dot_general(
                    part, part, (((0,), (0,)), ((), ())), preferred_element_type=f32
                )
                ones = jnp.ones((8, part.shape[0]), part.dtype)
                sums = sums + jnp.dot(ones, part, preferred_element_type=f32)
        half = left(share)

        def cell(r, h):
            return total[share * r : share * (r + 1), LANES * h : LANES * (h + 1)]

        main = (
            cell(0, 0),
            jnp.where(half, cell(1, 1), cell(1, 0)),
            cell(2, 1),
            jnp.where(half, cell(3, 0), cell(3, 1)),
        )
        across = jnp.where(half, cell(0, 1), cell(1, 1))
        for b in range(4):
            pack[i, b, 0:share] = main[b]
            pack[i, b, share:rows] = across[quarter * b : quarter * (b + 1)]
        line = lax.broadcasted_iota(jnp.int32, (24, width), 0)
        lane = lax.broadcasted_iota(jnp.int32, (24, width), 1)
        kept = jnp.where(line == t, sums[0:1], own_s[...])
        number = jnp.full((24, width), count, jnp.int32).astype(f32)
        own_s[...] = jnp.where((line == days) & (lane == t), number, kept)

    def block(i, k):
        return lax.rem(z + (nz - step_of(i)) * (k + 1), nz)

    def send(i, k):
        return pltpu.make_async_remote_copy(
            src_ref=pack.at[i, block(i, 0)] if k == 0 else hop.at[k - 1, i],
            dst_ref=hop.at[k, i],
            send_sem=hop_send.at[k, i],
            recv_sem=hop_recv.at[k, i],
            device_id=peer(step_of(i)),
            device_id_type=MESH,
        )

    def advance(i, k):
        send(i, k - 1).wait_recv()
        hop[k - 1, i] = hop[k - 1, i] + pack[i, block(i, k)]
        send(i, k).start()

    def give_to(i, j):
        start, size, land = ((0, 40, 0), (40, 8, 48), (32, 8, 40))[j - 1]
        return pltpu.make_async_remote_copy(
            src_ref=give.at[i, pl.ds(start, size)],
            dst_ref=take.at[i, pl.ds(land, size)],
            send_sem=give_send.at[j - 1, i],
            recv_sem=give_recv.at[j - 1, i],
            device_id=peer(j),
            device_id_type=MESH,
        )

    def reduce_last(i):
        send(i, 2).wait_recv()
        mine = hop[2, i] + pack[i, z]
        hop[2, i] = mine
        both = flipped(mine[0:share])
        turn = jnp.where(even, both[share:], both[:share])
        edge = mine[share:rows]
        edge_t = turned(edge)
        half8 = left(8)
        lefts = jnp.where(half8, edge[0:8], edge_t[8:16])
        rights = jnp.where(half8, edge_t[0:8], edge[8:16])
        give[i, 0:low32] = jnp.where(left(low32), turn[0:low32], turn[low32:])
        give[i, 32:40] = jnp.where(even, rights, lefts)
        give[i, 40:48] = jnp.where(even, lefts, rights)
        for j in range(1, nz):
            give_to(i, j).start()

    def halo(i):
        side = i // HALF
        return pltpu.make_async_remote_copy(
            src_ref=ext.at[day_of(i) + HALF],
            dst_ref=ext.at[i + days * side],
            send_sem=halo_send.at[i],
            recv_sem=halo_recv.at[i],
            device_id={"day": lax.rem(q + 1 + (nq - 2) * side, nq)},
            device_id_type=MESH,
        )

    def add_day(e):
        value = ext[e]

        def one(k, carry):
            acc[e + k] = acc[e + k] + value
            return carry

        lax.fori_loop(0, SPAN, one, 0)

    def assemble(i):
        for j in range(1, nz):
            give_to(i, j).wait_recv()
        pieces = (give[i, 40:48], take[i, 40:48], take[i, 48:56], take[i, 32:40])
        for j, piece in enumerate(pieces):
            at = quarter * lax.rem(z + j, nz)
            tile[pl.ds(pl.multiple_of(at, 8), 8)] = piece
            tile[pl.ds(pl.multiple_of(at + 8, 8), 8)] = turned(piece)
        flat = tile[...]
        straight = jnp.where(z == 0, flat, turned(flat))
        opposite = jnp.where(z < 2, straight, flipped(flat)[:share])
        near_p = take[i, 0:32]
        near_t = turned(near_p)
        beside = jnp.where(
            even,
            jnp.concatenate([near_t, near_p], axis=0),
            jnp.concatenate([near_p, near_t], axis=0),
        )
        lane = lax.broadcasted_iota(jnp.int32, (share, LANES), 1) // (LANES // 2)
        other = jnp.where(lane == lax.rem(z, 2), opposite, beside)
        left_main = 1 - lax.rem((z + 1) // 2, 2)
        right_main = 1 - z // 2
        use = jnp.where(lane == 0, left_main, right_main) == 1
        main = hop[2, i, 0:share]
        e = day_of(i) + HALF
        ext[e, :, 0:LANES] = jnp.where(use, main, other)
        ext[e, :, LANES:] = jnp.where(use, other, main)

        @pl.when(i < 2 * HALF)
        def _():
            halo(i).start()

        add_day(e)

    def add_halo(i):
        halo(i).wait_recv()
        add_day(i + days * (i // HALF))

    def put(d):
        return pltpu.make_async_copy(acc.at[d + 2 * HALF], out_ref.at[d], o_sem.at[d])

    def close(d):
        scale = inv_s[d][0:1]
        acc[d + 2 * HALF, :, 0:LANES] = acc[d + 2 * HALF, :, 0:LANES] * scale
        acc[d + 2 * HALF, :, LANES:] = acc[d + 2 * HALF, :, LANES:] * scale
        put(d).start()

    compute(0)
    pl.semaphore_wait(barrier, nz + 1)
    send(0, 0).start()

    def first(v, carry):
        compute(v)
        send(v, 0).start()

        @pl.when(v >= LAG1)
        def _():
            advance(v - LAG1, 1)

        return carry

    lax.fori_loop(1, days, first, 0)

    def share_sums(j):
        return pltpu.make_async_remote_copy(
            src_ref=own_s,
            dst_ref=got_s.at[j - 1],
            send_sem=sum_send.at[j - 1],
            recv_sem=sum_recv.at[j - 1],
            device_id=peer(j),
            device_id_type=MESH,
        )

    for j in range(1, nz):
        share_sums(j).start()

    stages = (
        (LAG1 - days, days - LAG1, days, lambda i: advance(i, 1)),
        (0, 0, days, lambda i: advance(i, 2)),
        (LAG3, 0, days, reduce_last),
        (LAG4, 0, days, assemble),
        (LAG5, 0, 2 * HALF, add_halo),
        (LAG4 + 2 * HALF, 0, HALF + 1, close),
    )

    def run(begin, end):
        def body(v, carry):
            for lag, lo, hi, stage in stages:
                i = v - lag
                if end - lag <= lo or begin - lag >= hi:
                    continue
                if begin - lag >= lo and end - lag <= hi:
                    stage(i)
                else:
                    pl.when((i >= lo) & (i < hi))(functools.partial(stage, i))
            return carry

        lax.fori_loop(begin, end, body, 0)

    def near(side):
        at = pl.ds(last if side == 0 else 0, 8)
        return pltpu.make_async_remote_copy(
            src_ref=mrg_s.at[at],
            dst_ref=near_s.at[side],
            send_sem=near_send.at[side],
            recv_sem=near_recv.at[side],
            device_id=after if side == 0 else before,
            device_id_type=MESH,
        )

    run(0, 5)
    for j in range(1, nz):
        share_sums(j).wait()
    merged = own_s[...]
    for j in range(1, nz):
        merged = merged + got_s[j - 1]
    line = lax.broadcasted_iota(jnp.int32, (24, LANES), 0)
    lane = lax.broadcasted_iota(jnp.int32, (24, LANES), 1)
    number = jnp.where(line == lane, merged[days : days + 1, 0:LANES], 0.0)
    number = jnp.sum(number, axis=1, keepdims=True)
    mrg_s[:, 0:width] = merged
    mrg_s[:, width:] = jnp.broadcast_to(number, (24, LANES))
    for side in range(2):
        near(side).start()
    ext_s[HALF : HALF + days] = mrg_s[0:days]

    run(5, 10)
    for side in range(2):
        near(side).wait()
    ext_s[0:HALF] = near_s[0, 0:HALF]
    ext_s[HALF + days : 2 * HALF + days] = near_s[1, 0:HALF]
    win = ext_s[0:24]
    for k in range(1, SPAN):
        win = win + ext_s[k : k + 24]
    win_sum = win[:, 0:width]
    win_count = win[:, width:]
    mean_s[:, 0:LANES] = win_sum[:, 0:LANES] / win_count
    mean_s[:, LANES:] = win_sum[:, LANES:] / win_count
    inverse = 1.0 / (win_count - 1.0)
    own = mean_s[:, pl.ds(pl.multiple_of(LANES * (z // 2), LANES), LANES)]
    own = jnp.where(even, own, turned(own))
    own_m[...] = own
    mean_copy = pltpu.make_async_copy(own_m, mean_ref, m_sem)
    mean_copy.start()
    column = jnp.concatenate([own, jnp.zeros((LANES - 24, LANES), f32)], axis=0).T[:share]
    for d in range(days):
        inv_s[d] = jnp.broadcast_to(inverse[d : d + 1], (8, LANES))
        outer = column[:, d : d + 1] * win_sum[d : d + 1]
        acc[d + 2 * HALF] = acc[d + 2 * HALF] - outer

    run(10, days + LAG4)

    def rest(d, carry):
        close(d)
        return carry

    lax.fori_loop(HALF + 1, days, rest, 0)

    def drain(i, carry):
        for k in range(nz - 1):
            send(i, k).wait_send()
            give_to(i, k + 1).wait_send()
        return carry

    lax.fori_loop(0, days, drain, 0)

    def drain_halo(i, carry):
        halo(i).wait_send()
        return carry

    lax.fori_loop(0, 2 * HALF, drain_halo, 0)
    mean_copy.wait()

    def written(d, carry):
        put(d).wait()
        return carry

    lax.fori_loop(0, days, written, 0)


def shards(samples, counts):
    days, groups, slots, width = samples.shape
    nz = lax.axis_size("year")
    share = width // nz
    rows = share + share // nz
    low = slots // 2 // 16 * 16
    f32 = jnp.float32
    dma = pltpu.SemaphoreType.DMA
    covariance, mean = pl.pallas_call(
        functools.partial(kernel, low),
        out_shape=(
            jax.ShapeDtypeStruct((days, share, width), f32),
            jax.ShapeDtypeStruct((24, LANES), f32),
        ),
        in_specs=[pl.BlockSpec(memory_space=pl.ANY), pl.BlockSpec(memory_space=pl.ANY)],
        out_specs=(pl.BlockSpec(memory_space=pl.ANY), pl.BlockSpec(memory_space=pl.ANY)),
        scratch_shapes=[
            pltpu.SMEM((groups, days), jnp.int32),
            pltpu.VMEM((SLOTS, groups, slots, width), samples.dtype),
            pltpu.VMEM((days, nz, rows, LANES), f32),
            pltpu.VMEM((nz - 1, days, rows, LANES), f32),
            pltpu.VMEM((days, 48, LANES), f32),
            pltpu.VMEM((days, 56, LANES), f32),
            pltpu.VMEM((share, LANES), f32),
            pltpu.VMEM((days + 2 * HALF, share, width), f32),
            pltpu.VMEM((days + 4 * HALF, share, width), f32),
            pltpu.VMEM((24, width), f32),
            pltpu.VMEM((nz - 1, 24, width), f32),
            pltpu.VMEM((24, width + LANES), f32),
            pltpu.VMEM((2, 8, width + LANES), f32),
            pltpu.VMEM((40, width + LANES), f32),
            pltpu.VMEM((24, width), f32),
            pltpu.VMEM((days, 8, LANES), f32),
            pltpu.VMEM((24, LANES), f32),
            dma,
            dma((SLOTS,)),
            dma((days,)),
            dma,
            dma((nz - 1, days)),
            dma((nz - 1, days)),
            dma((nz - 1, days)),
            dma((nz - 1, days)),
            dma((2 * HALF,)),
            dma((2 * HALF,)),
            dma((nz - 1,)),
            dma((nz - 1,)),
            dma((2,)),
            dma((2,)),
        ],
        compiler_params=pltpu.CompilerParams(
            collective_id=0, has_side_effects=True, vmem_limit_bytes=56 * 2**20
        ),
    )(jnp.swapaxes(counts, 1, 2)[0], samples)
    return (covariance[None], mean[:days, :share][None])


def solution(mesh):
    placed = (P("day", "year", "region", None), P("region", "day", "year"))
    return jax.shard_map(
        shards,
        mesh=mesh,
        in_specs=placed,
        out_specs=(P("region", "day", "year", None), P("region", "day", "year")),
        check_vma=False,
    )
```

time: 70.9 us -> 69.4 us (0.979)
  other arithmetic: 3.73 us -> 0 us
  Pallas kernels: 63.4 us -> 64.6 us
  local copies, waits for them, and re-layouts: 2.79 us -> 3.97 us
    broadcast_in_dim x1 -> x0, other arithmetic: 2.84 us -> none  [shards(): return (covariance[None], own_mean[None])]
    unnamed x1 -> x2, local copies, waits for them, and re-layouts: 1.36 us -> 3.27 us
    pallas_call x1, Pallas kernels: 63.4 us -> 64.6 us  [shards(): pl.pallas_call(functools.partial(kernel, low), out_shape=(jax.ShapeDtypeS...]
    slice x1 -> x0, local copies, waits for them, and re-layouts: 0.82 us -> none  [shards(): win_count = win[:days, width]]
    div x1 -> x0, other arithmetic: 0.82 us -> none  [shards(): full_mean = win_sum / win_count[:, None]]
where the time goes in v2:
time: 69.4 us; the launch traced here: 69.2 us
  Pallas kernels  64.6 us (93%)
  local copies, waits for them, and re-layouts  3.97 us (6%)
    pallas_call x1, Pallas kernels, shards(): pl.pallas_call(functools.partial(kernel, low), out_shape=(jax.ShapeDtypeS...  64.6 us
    unnamed x2, local copies, waits for them, and re-layouts  3.27 us

profile of v2, /device:TPU:0, one launch (start us, length us, event | category | flops | bytes accessed | tf_op | source)
XLA Modules:
  0.0 69.2 jit_solution(16357663778672923488)
XLA Ops:
  0.6 64.6 %shard_map.41 = (f32[23,64,256]{2,1,0:T(8,128)}, f32[24,128]{1,0:T(8,128)}) custom-call(s32[2,23]{1,0:T(2,128)} %bitcast.7, bf16[23,2,1000,256]{3,2,1,0:T(8,128)(2,1)} %x_ref.1), custom_call_target="tpu_custom_call" | custom-call | tf_op jit(solution)/shard_map/pallas_call | solution.py:419
  65.2 0.7 %slice_bitcast_fusion = f32[1,23,64]{2,1,0:T(8,128)S(1)} fusion(f32[24,128]{1,0:T(8,128)} %get-tuple-element.5), kind=kLoop, calls=%fused_computation | loop fusion | bytes 11776 | tf_op jit(solution)/shard_map/broadcast_in_dim | solution.py:464
  66.0 0.6 copy.4
  66.6 2.7 %copy.6 = f32[1,23,64,256]{3,2,1,0:T(8,128)} copy(f32[1,23,64,256]{3,2,1,0:T(8,128)} %bitcast.6) | data formatting | bytes 3014656

commit v3 on v2

--- a/solution.py
+++ b/solution.py
@@ -9,13 +9,13 @@
 
 HALF = 7
 SPAN = 2 * HALF + 1
-SLOTS = 4
-AHEAD = 3
+SLOTS = 8
+AHEAD = 7
 LANES = 128
-LAG1 = 4
-LAG3 = 3
-LAG4 = 6
-LAG5 = 11
+LAG1 = 8
+LAG3 = 6
+LAG4 = 12
+LAG5 = 17
 MESH = pl.DeviceIdType.MESH
 
 
@@ -139,18 +139,19 @@
                 total = total + lax.dot_general(
                     part, part, (((0,), (0,)), ((), ())), preferred_element_type=f32
                 )
-                ones = jnp.ones((8, part.shape[0]), part.dtype)
-                sums = sums + jnp.dot(ones, part, preferred_element_type=f32)
+                sums = sums + jnp.sum(part.astype(f32).reshape(-1, 8, width), axis=0)
         half = left(share)
 
         def cell(r, h):
             return total[share * r : share * (r + 1), LANES * h : LANES * (h + 1)]
 
+        lane_no = lax.broadcasted_iota(jnp.int32, (share, LANES), 1)
+        wide = lane_no * 0 + step_of(i) == 1
         main = (
-            cell(0, 0),
-            jnp.where(half, cell(1, 1), cell(1, 0)),
-            cell(2, 1),
-            jnp.where(half, cell(3, 0), cell(3, 1)),
+            jnp.where(half | wide, cell(0, 0), cell(0, 1)),
+            jnp.where(half & wide, cell(1, 1), cell(1, 0)),
+            jnp.where(half | wide, cell(2, 1), cell(2, 0)),
+            jnp.where(half & wide, cell(3, 0), cell(3, 1)),
         )
         across = jnp.where(half, cell(0, 1), cell(1, 1))
         for b in range(4):
@@ -158,7 +159,7 @@
             pack[i, b, share:rows] = across[quarter * b : quarter * (b + 1)]
         line = lax.broadcasted_iota(jnp.int32, (24, width), 0)
         lane = lax.broadcasted_iota(jnp.int32, (24, width), 1)
-        kept = jnp.where(line == t, sums[0:1], own_s[...])
+        kept = jnp.where(line == t, jnp.sum(sums, axis=0, keepdims=True), own_s[...])
         number = jnp.full((24, width), count, jnp.int32).astype(f32)
         own_s[...] = jnp.where((line == days) & (lane == t), number, kept)
 
@@ -182,12 +183,13 @@
 
     def give_to(i, j):
         start, size, land = ((0, 40, 0), (40, 8, 48), (32, 8, 40))[j - 1]
+        to = (step_of(i), 2, nz - step_of(i))[j - 1]
         return pltpu.make_async_remote_copy(
             src_ref=give.at[i, pl.ds(start, size)],
             dst_ref=take.at[i, pl.ds(land, size)],
             send_sem=give_send.at[j - 1, i],
             recv_sem=give_recv.at[j - 1, i],
-            device_id=peer(j),
+            device_id=peer(to),
             device_id_type=MESH,
         )
 
@@ -232,7 +234,8 @@
         for j in range(1, nz):
             give_to(i, j).wait_recv()
         pieces = (give[i, 40:48], take[i, 40:48], take[i, 48:56], take[i, 32:40])
-        for j, piece in enumerate(pieces):
+        s = step_of(i)
+        for j, piece in zip((0, s, 2, nz - s), pieces):
             at = quarter * lax.rem(z + j, nz)
             tile[pl.ds(pl.multiple_of(at, 8), 8)] = piece
             tile[pl.ds(pl.multiple_of(at + 8, 8), 8)] = turned(piece)
@@ -248,9 +251,9 @@
         )
         lane = lax.broadcasted_iota(jnp.int32, (share, LANES), 1) // (LANES // 2)
         other = jnp.where(lane == lax.rem(z, 2), opposite, beside)
-        left_main = 1 - lax.rem((z + 1) // 2, 2)
-        right_main = 1 - z // 2
-        use = jnp.where(lane == 0, left_main, right_main) == 1
+        own_main = 1 - z // 2
+        next_main = 1 - lax.rem(z + s, nz) // 2
+        use = jnp.where(lane == lax.rem(z, 2), own_main, next_main) == 1
         main = hop[2, i, 0:share]
         e = day_of(i) + HALF
         ext[e, :, 0:LANES] = jnp.where(use, main, other)
@@ -304,8 +307,13 @@
     for j in range(1, nz):
         share_sums(j).start()
 
+    def second(v, carry):
+        advance(v, 1)
+        return carry
+
+    lax.fori_loop(days - LAG1, days, second, 0)
+
     stages = (
-        (LAG1 - days, days - LAG1, days, lambda i: advance(i, 1)),
         (0, 0, days, lambda i: advance(i, 2)),
         (LAG3, 0, days, reduce_last),
         (LAG4, 0, days, assemble),
@@ -338,7 +346,7 @@
             device_id_type=MESH,
         )
 
-    run(0, 5)
+    run(0, 8)
     for j in range(1, nz):
         share_sums(j).wait()
     merged = own_s[...]
@@ -354,7 +362,7 @@
         near(side).start()
     ext_s[HALF : HALF + days] = mrg_s[0:days]
 
-    run(5, 10)
+    run(8, 16)
     for side in range(2):
         near(side).wait()
     ext_s[0:HALF] = near_s[0, 0:HALF]
@@ -369,7 +377,8 @@
     inverse = 1.0 / (win_count - 1.0)
     own = mean_s[:, pl.ds(pl.multiple_of(LANES * (z // 2), LANES), LANES)]
     own = jnp.where(even, own, turned(own))
-    own_m[...] = own
+    for d in range(days):
+        own_m[d] = own[d : d + 1, 0:share]
     mean_copy = pltpu.make_async_copy(own_m, mean_ref, m_sem)
     mean_copy.start()
     column = jnp.concatenate([own, jnp.zeros((LANES - 24, LANES), f32)], axis=0).T[:share]
@@ -378,7 +387,7 @@
         outer = column[:, d : d + 1] * win_sum[d : d + 1]
         acc[d + 2 * HALF] = acc[d + 2 * HALF] - outer
 
-    run(10, days + LAG4)
+    run(16, days + LAG4)
 
     def rest(d, carry):
         close(d)
@@ -406,6 +415,15 @@
         return carry
 
     lax.fori_loop(0, days, written, 0)
+
+
+def hand_over(cov_ref, mean_ref, cov_out, mean_out, cov_sem, mean_sem):
+    big = pltpu.make_async_copy(cov_ref, cov_out, cov_sem)
+    small = pltpu.make_async_copy(mean_ref, mean_out, mean_sem)
+    big.start()
+    small.start()
+    big.wait()
+    small.wait()
 
 
 def shards(samples, counts):
@@ -420,9 +438,9 @@
         functools.partial(kernel, low),
         out_shape=(
             jax.ShapeDtypeStruct((days, share, width), f32),
-            jax.ShapeDtypeStruct((24, LANES), f32),
+            jax.ShapeDtypeStruct((days, 1, share), f32),
         ),
-        in_specs=[pl.BlockSpec(memory_space=pl.ANY), pl.BlockSpec(memory_space=pl.ANY)],
+        in_specs=[pl.BlockSpec(memory_space=pltpu.HBM), pl.BlockSpec(memory_space=pltpu.HBM)],
         out_specs=(pl.BlockSpec(memory_space=pl.ANY), pl.BlockSpec(memory_space=pl.ANY)),
         scratch_shapes=[
             pltpu.SMEM((groups, days), jnp.int32),
@@ -441,7 +459,7 @@
             pltpu.VMEM((40, width + LANES), f32),
             pltpu.VMEM((24, width), f32),
             pltpu.VMEM((days, 8, LANES), f32),
-            pltpu.VMEM((24, LANES), f32),
+            pltpu.VMEM((days, 1, share), f32),
             dma,
             dma((SLOTS,)),
             dma((days,)),
@@ -458,10 +476,21 @@
             dma((2,)),
         ],
         compiler_params=pltpu.CompilerParams(
-            collective_id=0, has_side_effects=True, vmem_limit_bytes=56 * 2**20
+            collective_id=0, has_side_effects=True, vmem_limit_bytes=44 * 2**20
         ),
     )(jnp.swapaxes(counts, 1, 2)[0], samples)
-    return (covariance[None], mean[:days, :share][None])
+    covariance, mean = pl.pallas_call(
+        hand_over,
+        out_shape=(
+            jax.ShapeDtypeStruct((days, share, width), f32),
+            jax.ShapeDtypeStruct((days, 1, share), f32),
+        ),
+        in_specs=[pl.BlockSpec(memory_space=pl.ANY), pl.BlockSpec(memory_space=pl.ANY)],
+        out_specs=(pl.BlockSpec(memory_space=pl.ANY), pl.BlockSpec(memory_space=pl.ANY)),
+        scratch_shapes=[dma, dma],
+        compiler_params=pltpu.CompilerParams(vmem_limit_bytes=2**20),
+    )(covariance, mean)
+    return (covariance[None], jnp.swapaxes(mean, 0, 1))
 
 
 def solution(mesh):

time: 69.4 us -> 58.9 us (0.85)
  Pallas kernels: 64.6 us -> 57 us
  local copies, waits for them, and re-layouts: 3.97 us -> 0.67 us
    pallas_call x1, Pallas kernels: 64.6 us -> 55.8 us  [shards(): pl.pallas_call(functools.partial(kernel, low), out_shape=(jax.ShapeDtypeS...]
    unnamed x2, local copies, waits for them, and re-layouts: 3.27 us -> 0.67 us
    pallas_call x0 -> x1, Pallas kernels: none -> 1.14 us  [shards(): pl.pallas_call(hand_over, out_shape=(jax.ShapeDtypeStruct((days, share, w...]
    broadcast_in_dim x1 -> x0, local copies, waits for them, and re-layouts: 0.71 us -> none  [shards(): return (covariance[None], mean[:days, :share][None])]
where the time goes in v3:
time: 58.9 us; the launch traced here: 58.3 us
  Pallas kernels  57 us (97%)
  local copies, waits for them, and re-layouts  0.67 us (1%)
  between operations  0.65 us (1%)
    pallas_call x1, Pallas kernels, shards(): pl.pallas_call(functools.partial(kernel, low), out_shape=(jax.ShapeDtypeS...  55.8 us

profile of v3, /device:TPU:0, one launch (start us, length us, event | category | flops | bytes accessed | tf_op | source)
XLA Modules:
  0.0 58.3 jit_solution(10511493818929814596)
XLA Ops:
  0.6 0.0 copy-start
  0.6 0.7 %copy-done = s32[1,23,2]{1,2,0:T(2,128)S(1)} copy-done((s32[1,23,2]{1,2,0:T(2,128)S(1)}, s32[1,23,2]{1,2,0:T(2,128)}, u32[]{:S(2)}) %copy-start) | copy-done | bytes 208
  1.3 55.8 %shard_map.41 = (f32[23,64,256]{2,1,0:T(8,128)S(1)}, f32[23,1,64]{2,1,0:T(1,128)S(1)}) custom-call(s32[2,23]{1,0:T(2,128)S(1)} %bitcast.5, bf16[23,2,1000,256]{3,2,1,0:T(8,128)(2,1)} %x_ref.1), custom_call_target="tpu_custom_call" | custom-call | tf_op jit(solution)/shard_map/pallas_call | solution.py:437
  57.1 1.1 %shard_map.42 = (f32[23,64,256]{2,1,0:T(8,128)}, f32[23,1,64]{2,1,0:T(1,128)}) custom-call(f32[23,64,256]{2,1,0:T(8,128)S(1)} %get-tuple-element.6.cov_ref, f32[23,1,64]{2,1,0:T(1,128)S(1)} %get-tuple-element.7.mean_ref), custom_call_target="tpu_custom_call" | custom-call | tf_op jit(solution)/shard_map/pallas_call | solution.py:482
Async XLA Ops:
  0.6 0.7 %copy-start = (s32[1,23,2]{1,2,0:T(2,128)S(1)}, s32[1,23,2]{1,2,0:T(2,128)}, u32[]{:S(2)}) copy-start(s32[1,23,2]{1,2,0:T(2,128)} %param.3) | copy-start | bytes 556

commit v4 on v3

--- a/solution.py
+++ b/solution.py
@@ -49,11 +49,8 @@
     ext_s,
     mean_s,
     inv_s,
-    own_m,
     c_sem,
     x_sem,
-    o_sem,
-    m_sem,
     hop_send,
     hop_recv,
     give_send,
@@ -73,7 +70,7 @@
     nq = lax.axis_size("day")
     share = width // nz
     quarter = share // nz
-    rows = share + quarter
+    rows = share + quarter // 2
     low32 = share // 2
     last = days - HALF
     even = lax.rem(z, 2) == 0
@@ -104,8 +101,8 @@
 
     counted = pltpu.make_async_copy(cnt_ref, cnt, c_sem)
     counted.start()
-    for i in range(AHEAD):
-        fetch(i).start()
+    fetch(0).start()
+    fetch(1).start()
     own_s[...] = jnp.zeros_like(own_s)
     ext_s[...] = jnp.zeros_like(ext_s)
 
@@ -116,14 +113,18 @@
     lax.fori_loop(0, days + 4 * HALF, clear, 0)
     counted.wait()
 
-    def compute(i):
+    def compute(i, opening=False):
         slot = lax.rem(i, SLOTS)
         t = day_of(i)
         fetch(i).wait()
-
-        @pl.when(i + AHEAD < days)
-        def _():
-            fetch(i + AHEAD).start()
+        if opening:
+            for j in range(2, AHEAD + 1):
+                fetch(j).start()
+        else:
+
+            @pl.when(i + AHEAD < days)
+            def _():
+                fetch(i + AHEAD).start()
 
         total = jnp.zeros((width, width), f32)
         sums = jnp.zeros((8, width), f32)
@@ -154,9 +155,19 @@
             jnp.where(half & wide, cell(3, 0), cell(3, 1)),
         )
         across = jnp.where(half, cell(0, 1), cell(1, 1))
+        gap = lax.broadcasted_iota(jnp.int32, (low32, LANES), 1) // 32
         for b in range(4):
-            pack[i, b, 0:share] = main[b]
-            pack[i, b, share:rows] = across[quarter * b : quarter * (b + 1)]
+            spare = across[quarter * b + 8 : quarter * (b + 1)]
+            start = (b % 2) * (LANES // 2)
+            strips = [
+                spare if (start - 32 * k) % LANES == 0 else pltpu.roll(spare, (start - 32 * k) % LANES, 1)
+                for k in range(4)
+            ]
+            pack[i, b, 0:low32] = main[b][0:low32]
+            pack[i, b, low32:share] = jnp.where(
+                gap == 2 * (b % 2), jnp.concatenate(strips, axis=0), main[b][low32:]
+            )
+            pack[i, b, share:rows] = across[quarter * b : quarter * b + 8]
         line = lax.broadcasted_iota(jnp.int32, (24, width), 0)
         lane = lax.broadcasted_iota(jnp.int32, (24, width), 1)
         kept = jnp.where(line == t, jnp.sum(sums, axis=0, keepdims=True), own_s[...])
@@ -196,10 +207,19 @@
     def reduce_last(i):
         send(i, 2).wait_recv()
         mine = hop[2, i] + pack[i, z]
-        hop[2, i] = mine
-        both = flipped(mine[0:share])
+        main = mine[0:share]
+        both = flipped(main)
         turn = jnp.where(even, both[share:], both[:share])
-        edge = mine[share:rows]
+        mirror = jnp.where(even, both[:share], both[share:])
+        lane32 = lax.broadcasted_iota(jnp.int32, (share, LANES), 1) // 32
+        deep = lax.broadcasted_iota(jnp.int32, (share, LANES), 0) >= low32
+        hop[2, i, 0:share] = jnp.where(deep & (lane32 == 2 * lax.rem(z, 2)), mirror, main)
+        strips = main[low32:]
+        strips = jnp.where(even, strips, turned(strips))
+        spare = strips[0:8]
+        for k in range(1, 4):
+            spare = jnp.where(lane32[0:8] == k, pltpu.roll(strips[8 * k : 8 * k + 8], 32 * k, 1), spare)
+        edge = jnp.concatenate([mine[share:rows], spare], axis=0)
         edge_t = turned(edge)
         half8 = left(8)
         lefts = jnp.where(half8, edge[0:8], edge_t[8:16])
@@ -269,16 +289,12 @@
         halo(i).wait_recv()
         add_day(i + days * (i // HALF))
 
-    def put(d):
-        return pltpu.make_async_copy(acc.at[d + 2 * HALF], out_ref.at[d], o_sem.at[d])
-
     def close(d):
         scale = inv_s[d][0:1]
-        acc[d + 2 * HALF, :, 0:LANES] = acc[d + 2 * HALF, :, 0:LANES] * scale
-        acc[d + 2 * HALF, :, LANES:] = acc[d + 2 * HALF, :, LANES:] * scale
-        put(d).start()
-
-    compute(0)
+        out_ref[d, :, 0:LANES] = acc[d + 2 * HALF, :, 0:LANES] * scale
+        out_ref[d, :, LANES:] = acc[d + 2 * HALF, :, LANES:] * scale
+
+    compute(0, True)
     pl.semaphore_wait(barrier, nz + 1)
     send(0, 0).start()
 
@@ -378,9 +394,7 @@
     own = mean_s[:, pl.ds(pl.multiple_of(LANES * (z // 2), LANES), LANES)]
     own = jnp.where(even, own, turned(own))
     for d in range(days):
-        own_m[d] = own[d : d + 1, 0:share]
-    mean_copy = pltpu.make_async_copy(own_m, mean_ref, m_sem)
-    mean_copy.start()
+        mean_ref[d] = own[d : d + 1, 0:share]
     column = jnp.concatenate([own, jnp.zeros((LANES - 24, LANES), f32)], axis=0).T[:share]
     for d in range(days):
         inv_s[d] = jnp.broadcast_to(inverse[d : d + 1], (8, LANES))
@@ -408,13 +422,6 @@
         return carry
 
     lax.fori_loop(0, 2 * HALF, drain_halo, 0)
-    mean_copy.wait()
-
-    def written(d, carry):
-        put(d).wait()
-        return carry
-
-    lax.fori_loop(0, days, written, 0)
 
 
 def hand_over(cov_ref, mean_ref, cov_out, mean_out, cov_sem, mean_sem):
@@ -430,7 +437,7 @@
     days, groups, slots, width = samples.shape
     nz = lax.axis_size("year")
     share = width // nz
-    rows = share + share // nz
+    rows = share + share // nz // 2
     low = slots // 2 // 16 * 16
     f32 = jnp.float32
     dma = pltpu.SemaphoreType.DMA
@@ -441,7 +448,7 @@
             jax.ShapeDtypeStruct((days, 1, share), f32),
         ),
         in_specs=[pl.BlockSpec(memory_space=pltpu.HBM), pl.BlockSpec(memory_space=pltpu.HBM)],
-        out_specs=(pl.BlockSpec(memory_space=pl.ANY), pl.BlockSpec(memory_space=pl.ANY)),
+        out_specs=(pl.BlockSpec(memory_space=pltpu.VMEM), pl.BlockSpec(memory_space=pltpu.VMEM)),
         scratch_shapes=[
             pltpu.SMEM((groups, days), jnp.int32),
             pltpu.VMEM((SLOTS, groups, slots, width), samples.dtype),
@@ -459,11 +466,8 @@
             pltpu.VMEM((40, width + LANES), f32),
             pltpu.VMEM((24, width), f32),
             pltpu.VMEM((days, 8, LANES), f32),
-            pltpu.VMEM((days, 1, share), f32),
             dma,
             dma((SLOTS,)),
-            dma((days,)),
-            dma,
             dma((nz - 1, days)),
             dma((nz - 1, days)),
             dma((nz - 1, days)),
@@ -478,7 +482,7 @@
         compiler_params=pltpu.CompilerParams(
             collective_id=0, has_side_effects=True, vmem_limit_bytes=44 * 2**20
         ),
-    )(jnp.swapaxes(counts, 1, 2)[0], samples)
+    )(pltpu.with_memory_space_constraint(jnp.swapaxes(counts, 1, 2)[0], pltpu.HBM), samples)
     covariance, mean = pl.pallas_call(
         hand_over,
         out_shape=(

time: 58.9 us -> 54.4 us (0.924)
  Pallas kernels: 57 us -> 53.5 us
  local copies, waits for them, and re-layouts: 0.67 us -> 0 us
    pallas_call x1, Pallas kernels: 55.8 us -> 52.3 us  [shards(): pl.pallas_call(functools.partial(kernel, low), out_shape=(jax.ShapeDtypeS...]
    unnamed x2 -> x0, local copies, waits for them, and re-layouts: 0.67 us -> none
where the time goes in v4:
time: 54.4 us; the launch traced here: 54.1 us
  Pallas kernels  53.5 us (98%)
  between operations  0.64 us (1%)
    pallas_call x1, Pallas kernels, shards(): pl.pallas_call(functools.partial(kernel, low), out_shape=(jax.ShapeDtypeS...  52.3 us
    pallas_call x1, Pallas kernels, shards(): pl.pallas_call(hand_over, out_shape=(jax.ShapeDtypeStruct((days, share, w...  1.14 us

profile of v4, /device:TPU:0, one launch (start us, length us, event | category | flops | bytes accessed | tf_op | source)
XLA Modules:
  0.0 54.1 jit_solution(15230172834278260170)
XLA Ops:
  0.6 52.3 %shard_map.41 = (f32[23,64,256]{2,1,0:T(8,128)S(1)}, f32[23,1,64]{2,1,0:T(1,128)S(1)}) custom-call(s32[2,23]{1,0:T(2,128)} %bitcast.5, bf16[23,2,1000,256]{3,2,1,0:T(8,128)(2,1)} %x_ref.1), custom_call_target="tpu_custom_call" | custom-call | tf_op jit(solution)/shard_map/pallas_call | solution.py:444
  53.0 1.1 %shard_map.42 = (f32[23,64,256]{2,1,0:T(8,128)}, f32[23,1,64]{2,1,0:T(1,128)}) custom-call(f32[23,64,256]{2,1,0:T(8,128)S(1)} %get-tuple-element.6.cov_ref, f32[23,1,64]{2,1,0:T(1,128)S(1)} %get-tuple-element.7.mean_ref), custom_call_target="tpu_custom_call" | custom-call | tf_op jit(solution)/shard_map/pallas_call | solution.py:486

commit v5 on v4

--- a/solution.py
+++ b/solution.py
@@ -15,7 +15,7 @@
 LAG1 = 8
 LAG3 = 6
 LAG4 = 12
-LAG5 = 17
+LAG5 = 20
 MESH = pl.DeviceIdType.MESH
 
 
@@ -248,7 +248,7 @@
             acc[e + k] = acc[e + k] + value
             return carry
 
-        lax.fori_loop(0, SPAN, one, 0)
+        lax.fori_loop(0, SPAN, one, 0, unroll=5)
 
     def assemble(i):
         for j in range(1, nz):

time: 54.4 us -> 53.7 us (0.987)
  Pallas kernels: 53.5 us -> 52.9 us
    pallas_call x1, Pallas kernels: 52.3 us -> 51.8 us  [shards(): pl.pallas_call(functools.partial(kernel, low), out_shape=(jax.ShapeDtypeS...]
where the time goes in v5:
time: 53.7 us; the launch traced here: 53.5 us
  Pallas kernels  52.9 us (99%)
  between operations  0.64 us (1%)
    pallas_call x1, Pallas kernels, shards(): pl.pallas_call(functools.partial(kernel, low), out_shape=(jax.ShapeDtypeS...  51.8 us
    pallas_call x1, Pallas kernels, shards(): pl.pallas_call(hand_over, out_shape=(jax.ShapeDtypeStruct((days, share, w...  1.14 us

profile of v5, /device:TPU:0, one launch (start us, length us, event | category | flops | bytes accessed | tf_op | source)
XLA Modules:
  0.0 53.5 jit_solution(15007465819602016343)
XLA Ops:
  0.6 51.8 %shard_map.41 = (f32[23,64,256]{2,1,0:T(8,128)S(1)}, f32[23,1,64]{2,1,0:T(1,128)S(1)}) custom-call(s32[2,23]{1,0:T(2,128)} %bitcast.5, bf16[23,2,1000,256]{3,2,1,0:T(8,128)(2,1)} %x_ref.1), custom_call_target="tpu_custom_call" | custom-call | tf_op jit(solution)/shard_map/pallas_call | solution.py:444
  52.4 1.1 %shard_map.42 = (f32[23,64,256]{2,1,0:T(8,128)}, f32[23,1,64]{2,1,0:T(1,128)}) custom-call(f32[23,64,256]{2,1,0:T(8,128)S(1)} %get-tuple-element.6.cov_ref, f32[23,1,64]{2,1,0:T(1,128)S(1)} %get-tuple-element.7.mean_ref), custom_call_target="tpu_custom_call" | custom-call | tf_op jit(solution)/shard_map/pallas_call | solution.py:486
